TPU v7x, 128 devices: a whole 4x4x4 slice. The times are simulated.
128 devices in a mesh: tmpl: 16 (over z, y_hi, core), chan: 8 (over y_lo, x).
Axes of the slice: x: 4, y: 4 (y_hi: 2, y_lo: 2; y = y_hi * 2 + y_lo), z: 4, core: 2. Of those that a mesh axis runs over, the one named last changes fastest.
Arguments:
- data: bfloat16 [16, 96, 2304], P('tmpl', 'chan')
- templates: bfloat16 [4096, 96, 200], P('tmpl', 'chan')
- counts: int32 [16], P('tmpl'), may hold values from 32 to 256, as said below
- owners: int32 [3], replicated, may hold values from 0 to 15
Outputs:
- traces: float32 [4096, 3, 2048], P('tmpl', None, 'chan')
Inputs may be any that keep to these rules, and one draw needn't show every extreme that they name: `counts`: every count is a multiple of 32; some index of tmpl holds exactly 256 live slots.
All inputs are finite; a program needn't handle non-finite values.
Results may differ from a plain program's by a relative error of at most 0.0041.
Values may be sent and summed in bfloat16 or wider, within the bound.
A program may use at most 128 MiB of HBM per device.

v0:
```python
import math

import jax
import jax.numpy as jnp
from jax import lax
from jax.sharding import PartitionSpec as P

W = 200
NB = 3
LO = 2048
TB = 32


eps_value = 1e-06


def sent_to_all(x, axis):
    copies = jnp.broadcast_to(x, (lax.axis_size(axis), *x.shape))
    return lax.all_to_all(copies, axis, split_axis=0, concat_axis=0, tiled=True)


def in_order(blocks, dim):
    blocks = jnp.moveaxis(blocks, 0, dim)
    dims = blocks.shape
    return blocks.reshape(*dims[:dim], dims[dim] * dims[dim + 1], *dims[dim + 2 :])


def gathered_copies(x, axis, dim):
    blocks = sent_to_all(x, axis)
    return in_order(blocks, dim)


def normalize_templates(templates):
    values = templates.astype(jnp.float32)
    spread = jnp.sqrt(jnp.mean(values * values, axis=-1, keepdims=True) + eps_value)
    scaled = (values / (spread * math.sqrt(values.shape[-1]))).astype(jnp.bfloat16)
    return scaled.reshape(values.shape[0], -1)


def scaled_windows(segment, window_len, lag_count):
    rows = segment.shape[0]
    length = segment.shape[1]
    period = length - 1
    tiled = jnp.tile(segment[:, :period], (1, window_len + 1))
    windows = (
        tiled[:, : window_len * length]
        .reshape(rows, window_len, length)[:, :, :lag_count]
        .astype(jnp.float32)
    )
    spread = jnp.sqrt(jnp.mean(windows * windows, axis=1, keepdims=True) + eps_value)
    scaled = (windows / (spread * math.sqrt(window_len))).astype(jnp.bfloat16)
    return scaled.reshape(-1, lag_count)


def channel_sum(partial_value):
    return lax.psum_scatter(partial_value, "chan", scatter_dimension=1, tiled=True)


def body(data, templates, counts, owners):
    normed = normalize_templates(templates)
    slot_cap = normed.shape[0]
    own_units = counts[0] // TB
    archive = gathered_copies(data, "tmpl", 0)
    results = []
    for number in range(NB):
        segment = lax.dynamic_index_in_dim(archive, owners[number], 0, keepdims=False)
        scaled = scaled_windows(segment, W, LO)

        def local_step(index, partial_value):
            tpl_rows = lax.dynamic_slice_in_dim(normed, index * TB, TB, 0)
            product = jnp.dot(tpl_rows, scaled, preferred_element_type=jnp.float32)
            return lax.dynamic_update_slice_in_dim(partial_value, product, index * TB, 0)

        partial_value = lax.fori_loop(
            jnp.int32(0), own_units, local_step, jnp.zeros((slot_cap, LO), jnp.float32)
        )
        results.append(channel_sum(partial_value))
    stacked = jnp.stack(results, axis=1)
    return stacked


def solution(mesh):
    placed = (P("tmpl", "chan", None), P("tmpl", "chan", None), P("tmpl"), P())
    return jax.shard_map(
        body, mesh=mesh, in_specs=placed, out_specs=P("tmpl", None, "chan"), check_vma=False
    )
```

profile of v0, /device:TPU:1, one launch (start us, length us, event | category | flops | bytes accessed | tf_op | source)
XLA Modules:
  0.0 446.0 jit_solution(4121846616795694883)
XLA Ops:
  8.5 9.4 %all-to-all-start = ((bf16[16,1,12,2304]{3,2,1,0:T(8,128)(2,1)}), bf16[16,1,12,2304]{3,2,1,0:T(8,128)(2,1)}, u32[]{:S(2)}, u32[]{:S(2)}) async-start(bf16[16,1,12,2304]{3,2,1,0:T(8,128)(2,1)} %broadcast_in_dim.2), calls=%async_computation | async-start | bytes 2359296 | tf_op jit(solution)/shard_map/all_to_all | solution.py:19
  29.9 6.6 %all-to-all-done = bf16[16,1,12,2304]{3,2,1,0:T(8,128)(2,1)} async-done(((bf16[16,1,12,2304]{3,2,1,0:T(8,128)(2,1)}), bf16[16,1,12,2304]{3,2,1,0:T(8,128)(2,1)}, u32[]{:S(2)}, u32[]{:S(2)}) %all-to-all-start) | async-done | bytes 884768 | tf_op jit(solution)/shard_map/all_to_all | solution.py:19
  37.5 5.0 %tile.14 = bf16[12,201,2303]{2,1,0:T(8,128)(2,1)} broadcast(bf16[12,2303]{1,0:T(8,128)(2,1)S(1)} %bitcast.55), dimensions={0,2} | broadcast | bytes 11164944 | tf_op jit(solution)/shard_map/tile | solution.py:44
  42.6 33.2 %tile.30 = bf16[12,462903]{1,0:T(8,128)(2,1)} reshape(bf16[12,201,2303]{2,1,0:T(8,128)(2,1)} %tile.14) | data formatting | bytes 22219344 | tf_op jit(solution)/shard_map/tile | solution.py:44
  75.7 5.2 %slice-done = bf16[12,460800]{1,0:T(8,128)(2,1)S(1)} async-done(((bf16[12,462903]{1,0:T(8,128)(2,1)}), bf16[12,460800]{1,0:T(8,128)(2,1)S(1)}, s32[]{:S(2)}) %slice-start) | async-done | bytes 11059224 | tf_op jit(solution)/shard_map/slice | solution.py:46
  80.9 8.5 %copy.10 = bf16[2,8,200,2304]{3,2,1,0:T(8,128)(2,1)} copy(bf16[2,8,200,2304]{3,1,2,0:T(8,128)(2,1)S(1)} %bitcast.46) | data formatting | bytes 29491200
  89.4 5.8 %slice.58 = bf16[12,200,2304]{2,1,0:T(8,128)(2,1)S(1)} slice(bf16[16,200,2304]{2,1,0:T(8,128)(2,1)} %bitcast.49), slice={[0:12], [0:200], [0:2304]} | slice | bytes 22118400 | tf_op jit(solution)/shard_map/reshape | solution.py:47
  95.2 4.2 copy-done.2
  101.5 11.2 %fusion.9 = bf16[12,200,2048]{2,1,0:T(8,128)(2,1)} fusion(f32[12,2048]{1,0:T(8,128)S(1)} %sqrt_multiply_fusion.1, bf16[12,200,2304]{2,1,0:T(8,128)(2,1)} %copy-done.2), kind=kLoop, calls=%fused_computation.18 | loop fusion | flops 14745600 | bytes 19759104 | tf_op jit(solution)/shard_map/convert_element_type | solution.py:51
  113.0 11.2 %while.31 = (s32[]{:T(128)}, f32[256,2048]{1,0:T(8,128)S(1)}, s32[]{:T(128)}, bf16[256,2400]{1,0:T(8,128)(2,1)S(1)}, bf16[2400,2048]{1,0:T(8,128)(2,1)}, /*index=5*/s32[]{:T(128)}, s32[]{:T(128)}, s32[]{:T(128)}, s32[]{:T(128)}) while((s32[]{:T(128)}, f32[256,2048]{1,0:T(8,128)S(1)}, s32[]{:T(128)}, bf16[256,2400]{1,0:T(8,128)(2,1)S(1)}, ...), condition=%wide.region_7.8_spmd, body=%wide.region_6.7_spmd.sunk | while | flops 314572800 | bytes 10249355 | solution.py:74
  113.0 5.6 %convolution_dynamic-update-slice_fusion.7 = f32[256,2048]{1,0:T(8,128)S(1)} fusion(f32[256,2048]{1,0:T(8,128)S(1)} %get-tuple-element.276, s32[]{:T(128)S(6)} %select_n.35, bf16[2400,2048]{1,0:T(8,128)(2,1)} %get-tuple-element.288, bf16[256,2400]{1,0:T(8,128)(2,1)S(1)} %get-tuple-element.287), kind=kOutput, calls=%fused_computation.3.clone.1 | convolution fusion | flops 314572800 | bytes 10249216 | tf_op jit(solution)/shard_map/while/body/dot_general | solution.py:71
  118.6 5.6 %convolution_dynamic-update-slice_fusion.7 = f32[256,2048]{1,0:T(8,128)S(1)} fusion(f32[256,2048]{1,0:T(8,128)S(1)} %get-tuple-element.276, s32[]{:T(128)S(6)} %select_n.35, bf16[2400,2048]{1,0:T(8,128)(2,1)} %get-tuple-element.288, bf16[256,2400]{1,0:T(8,128)(2,1)S(1)} %get-tuple-element.287), kind=kOutput, calls=%fused_computation.3.clone.1 | convolution fusion | flops 314572800 | bytes 10249216 | tf_op jit(solution)/shard_map/while/body/dot_general | solution.py:71
  125.6 5.0 %tile.12 = bf16[12,201,2303]{2,1,0:T(8,128)(2,1)} broadcast(bf16[12,2303]{1,0:T(8,128)(2,1)S(1)} %bitcast.54), dimensions={0,2} | broadcast | bytes 11164944 | tf_op jit(solution)/shard_map/tile | solution.py:44
  130.6 33.4 %tile.13 = bf16[12,462903]{1,0:T(8,128)(2,1)} reshape(bf16[12,201,2303]{2,1,0:T(8,128)(2,1)} %tile.12) | data formatting | bytes 22219344 | tf_op jit(solution)/shard_map/tile | solution.py:44
  164.0 5.3 %slice-done.1 = bf16[12,460800]{1,0:T(8,128)(2,1)S(1)} async-done(((bf16[12,462903]{1,0:T(8,128)(2,1)}), bf16[12,460800]{1,0:T(8,128)(2,1)S(1)}, s32[]{:S(2)}) %slice-start.1) | async-done | bytes 11059224 | tf_op jit(solution)/shard_map/slice | solution.py:46
  169.2 8.5 %copy.9 = bf16[2,8,200,2304]{3,2,1,0:T(8,128)(2,1)} copy(bf16[2,8,200,2304]{3,1,2,0:T(8,128)(2,1)S(1)} %bitcast.47) | data formatting | bytes 29491200
  177.7 5.8 %slice.57 = bf16[12,200,2304]{2,1,0:T(8,128)(2,1)S(1)} slice(bf16[16,200,2304]{2,1,0:T(8,128)(2,1)} %bitcast.50), slice={[0:12], [0:200], [0:2304]} | slice | bytes 22118400 | tf_op jit(solution)/shard_map/reshape | solution.py:47
  189.8 5.0 %tile.31 = bf16[12,201,2303]{2,1,0:T(8,128)(2,1)} broadcast(bf16[12,2303]{1,0:T(8,128)(2,1)S(1)} %bitcast.53), dimensions={0,2} | broadcast | bytes 11164944 | tf_op jit(solution)/shard_map/tile | solution.py:44
  194.8 33.0 %tile.32 = bf16[12,462903]{1,0:T(8,128)(2,1)} reshape(bf16[12,201,2303]{2,1,0:T(8,128)(2,1)} %tile.31) | data formatting | bytes 22219344 | tf_op jit(solution)/shard_map/tile | solution.py:44
  227.8 5.2 %slice-done.2 = bf16[12,460800]{1,0:T(8,128)(2,1)S(1)} async-done(((bf16[12,462903]{1,0:T(8,128)(2,1)}), bf16[12,460800]{1,0:T(8,128)(2,1)S(1)}, s32[]{:S(2)}) %slice-start.2) | async-done | bytes 11059224 | tf_op jit(solution)/shard_map/slice | solution.py:46
  233.0 8.5 %copy.11 = bf16[2,8,200,2304]{3,2,1,0:T(8,128)(2,1)} copy(bf16[2,8,200,2304]{3,1,2,0:T(8,128)(2,1)S(1)} %bitcast.48) | data formatting | bytes 29491200
  241.5 5.8 %slice.59 = bf16[12,200,2304]{2,1,0:T(8,128)(2,1)S(1)} slice(bf16[16,200,2304]{2,1,0:T(8,128)(2,1)} %bitcast.51), slice={[0:12], [0:200], [0:2304]} | slice | bytes 22118400 | tf_op jit(solution)/shard_map/reshape | solution.py:47
  253.6 11.2 %fusion.7 = bf16[12,200,2048]{2,1,0:T(8,128)(2,1)} fusion(f32[12,2048]{1,0:T(8,128)S(1)} %sqrt_multiply_fusion.2, bf16[12,200,2304]{2,1,0:T(8,128)(2,1)} %copy-done.1), kind=kLoop, calls=%fused_computation.16 | loop fusion | flops 14745600 | bytes 19759104 | tf_op jit(solution)/shard_map/convert_element_type | solution.py:51
  265.1 11.2 %while.30 = (s32[]{:T(128)}, f32[256,2048]{1,0:T(8,128)S(1)}, s32[]{:T(128)}, bf16[256,2400]{1,0:T(8,128)(2,1)S(1)}, bf16[2400,2048]{1,0:T(8,128)(2,1)}, /*index=5*/s32[]{:T(128)}, s32[]{:T(128)}, s32[]{:T(128)}, s32[]{:T(128)}) while((s32[]{:T(128)}, f32[256,2048]{1,0:T(8,128)S(1)}, s32[]{:T(128)}, bf16[256,2400]{1,0:T(8,128)(2,1)S(1)}, ...), condition=%wide.region_3.4_spmd, body=%wide.region_2.3_spmd.sunk | while | flops 314572800 | bytes 10249355 | solution.py:74
  265.1 5.6 %convolution_dynamic-update-slice_fusion.6 = f32[256,2048]{1,0:T(8,128)S(1)} fusion(f32[256,2048]{1,0:T(8,128)S(1)} %get-tuple-element.303, s32[]{:T(128)S(6)} %select_n.34, bf16[2400,2048]{1,0:T(8,128)(2,1)} %get-tuple-element.315, bf16[256,2400]{1,0:T(8,128)(2,1)S(1)} %get-tuple-element.314), kind=kOutput, calls=%fused_computation.clone.1 | convolution fusion | flops 314572800 | bytes 10249216 | tf_op jit(solution)/shard_map/while/body/dot_general | solution.py:71
  270.7 5.6 %convolution_dynamic-update-slice_fusion.6 = f32[256,2048]{1,0:T(8,128)S(1)} fusion(f32[256,2048]{1,0:T(8,128)S(1)} %get-tuple-element.303, s32[]{:T(128)S(6)} %select_n.34, bf16[2400,2048]{1,0:T(8,128)(2,1)} %get-tuple-element.315, bf16[256,2400]{1,0:T(8,128)(2,1)S(1)} %get-tuple-element.314), kind=kOutput, calls=%fused_computation.clone.1 | convolution fusion | flops 314572800 | bytes 10249216 | tf_op jit(solution)/shard_map/while/body/dot_general | solution.py:71
  277.7 11.2 %fusion.11 = bf16[12,200,2048]{2,1,0:T(8,128)(2,1)} fusion(f32[12,2048]{1,0:T(8,128)S(1)} %sqrt_multiply_fusion, bf16[12,200,2304]{2,1,0:T(8,128)(2,1)} %copy-done), kind=kLoop, calls=%fused_computation.20 | loop fusion | flops 14745600 | bytes 19759104 | tf_op jit(solution)/shard_map/convert_element_type | solution.py:51
  289.2 11.2 %while.32 = (s32[]{:T(128)}, f32[256,2048]{1,0:T(8,128)S(1)}, s32[]{:T(128)}, bf16[256,2400]{1,0:T(8,128)(2,1)S(1)}, bf16[2400,2048]{1,0:T(8,128)(2,1)}, /*index=5*/s32[]{:T(128)}, s32[]{:T(128)}, s32[]{:T(128)}, s32[]{:T(128)}) while((s32[]{:T(128)}, f32[256,2048]{1,0:T(8,128)S(1)}, s32[]{:T(128)}, bf16[256,2400]{1,0:T(8,128)(2,1)S(1)}, ...), condition=%wide.region_11.12_spmd, body=%wide.region_10.11_spmd.sunk | while | flops 314572800 | bytes 10249355 | solution.py:74
  289.2 5.6 %convolution_dynamic-update-slice_fusion.8 = f32[256,2048]{1,0:T(8,128)S(1)} fusion(f32[256,2048]{1,0:T(8,128)S(1)} %get-tuple-element.249, s32[]{:T(128)S(6)} %select_n.36, bf16[2400,2048]{1,0:T(8,128)(2,1)} %get-tuple-element.261, bf16[256,2400]{1,0:T(8,128)(2,1)S(1)} %get-tuple-element.260), kind=kOutput, calls=%fused_computation.6.clone.1 | convolution fusion | flops 314572800 | bytes 10249216 | tf_op jit(solution)/shard_map/while/body/dot_general | solution.py:71
  294.8 5.6 %convolution_dynamic-update-slice_fusion.8 = f32[256,2048]{1,0:T(8,128)S(1)} fusion(f32[256,2048]{1,0:T(8,128)S(1)} %get-tuple-element.249, s32[]{:T(128)S(6)} %select_n.36, bf16[2400,2048]{1,0:T(8,128)(2,1)} %get-tuple-element.261, bf16[256,2400]{1,0:T(8,128)(2,1)S(1)} %get-tuple-element.260), kind=kOutput, calls=%fused_computation.6.clone.1 | convolution fusion | flops 314572800 | bytes 10249216 | tf_op jit(solution)/shard_map/while/body/dot_general | solution.py:71
  301.8 77.3 %reduce-scatter.4.cloned.1.call-done = f32[256,256]{1,0:T(8,128)} async-done(((f32[256,2048]{1,0:T(8,128)}), f32[256,256]{1,0:T(8,128)}) %reduce-scatter.4.cloned.1.call-update) | async-done | bytes 262160 | tf_op jit(solution)/shard_map/reduce_scatter | solution.py:56
  379.1 58.2 %reduce-scatter.8.cloned.1.call-done = f32[256,256]{1,0:T(8,128)} async-done(((f32[256,2048]{1,0:T(8,128)}), f32[256,256]{1,0:T(8,128)}) %reduce-scatter.8.cloned.1.call-update) | async-done | bytes 262160 | tf_op jit(solution)/shard_map/reduce_scatter | solution.py:56
  (38 shorter events, 29.8 us)
Async XLA Ops:
  8.5 28.0 %all-to-all-start = ((bf16[16,1,12,2304]{3,2,1,0:T(8,128)(2,1)}), bf16[16,1,12,2304]{3,2,1,0:T(8,128)(2,1)}, u32[]{:S(2)}, u32[]{:S(2)}) async-start(bf16[16,1,12,2304]{3,2,1,0:T(8,128)(2,1)} %broadcast_in_dim.2), calls=%async_computation | async-start | bytes 2359296 | tf_op jit(solution)/shard_map/all_to_all | solution.py:19
  18.0 283.8 %reduce-scatter.6.cloned.1.call-start = ((), (), s32[]{:S(2)}) async-start(), calls=%async_computation.5 | async-start | bytes 2359296 | tf_op jit(solution)/shard_map/reduce_scatter | solution.py:56
  75.7 5.2 %slice-start = ((bf16[12,462903]{1,0:T(8,128)(2,1)}), bf16[12,460800]{1,0:T(8,128)(2,1)S(1)}, s32[]{:S(2)}) async-start(bf16[12,462903]{1,0:T(8,128)(2,1)} %tile.30), calls=%async_computation.7 | async-start | bytes 29491200 | tf_op jit(solution)/shard_map/slice | solution.py:46
  95.2 4.2 copy-start.2
  124.2 1.3 copy-start.4
  125.5 253.6 %reduce-scatter.4.cloned.1.call-start = ((), (), s32[]{:S(2)}) async-start(), calls=%async_computation.4 | async-start | bytes 2359296 | tf_op jit(solution)/shard_map/reduce_scatter | solution.py:56
  164.0 5.3 %slice-start.1 = ((bf16[12,462903]{1,0:T(8,128)(2,1)}), bf16[12,460800]{1,0:T(8,128)(2,1)S(1)}, s32[]{:S(2)}) async-start(bf16[12,462903]{1,0:T(8,128)(2,1)} %tile.13), calls=%async_computation.8 | async-start | bytes 29491200 | tf_op jit(solution)/shard_map/slice | solution.py:46
  183.6 4.1 copy-start.1
  227.8 5.2 %slice-start.2 = ((bf16[12,462903]{1,0:T(8,128)(2,1)}), bf16[12,460800]{1,0:T(8,128)(2,1)S(1)}, s32[]{:S(2)}) async-start(bf16[12,462903]{1,0:T(8,128)(2,1)} %tile.32), calls=%async_computation.9 | async-start | bytes 29491200 | tf_op jit(solution)/shard_map/slice | solution.py:46
  247.3 4.2 copy-start
  276.3 1.3 copy-start.5
  277.7 159.6 %reduce-scatter.8.cloned.1.call-start = ((), (), s32[]{:S(2)}) async-start(), calls=%async_computation.6 | async-start | bytes 2359296 | tf_op jit(solution)/shard_map/reduce_scatter | solution.py:56
  300.4 1.4 copy-start.3
Sparse Core Ops, SparseCore 0:
  125.6 67.6 reduce-scatter.5
  277.8 101.2 reduce-scatter.3
  381.5 55.6 reduce-scatter.7
where the time goes:
time: 455 us; the launch traced here: 446 us
  local copies, waits for them, and re-layouts  196 us (43%)
  waiting for transfers between devices  142 us (31%)
  other arithmetic  45 us (10%)
  matrix products  33.6 us (7%)
  between operations  20 us (4%)
  starting transfers between devices  9.57 us (2%)
    reduce_scatter x3, waiting for transfers between devices, channel_sum(): lax.psum_scatter(partial_value, 'chan', scatter_dimension=1, tiled=True)  135 us
    another operation x6, local copies, waits for them, and re-layouts, scaled_windows(): tiled = jnp.tile(segment[:, :period], (1, window_len + 1))  115 us
    unnamed x15, local copies, waits for them, and re-layouts  42 us
    dot_general x6, matrix products, local_step(): product = jnp.dot(tpl_rows, scaled, preferred_element_type=jnp.float32)  33.6 us
    convert_element_type x3, other arithmetic, scaled_windows(): scaled = (windows / (spread * math.sqrt(window_len))).astype(jnp.bfloat16)  33.6 us
    reshape x3, local copies, waits for them, and re-layouts, scaled_windows(): windows = tiled[:, :window_len * length].reshape(rows, window_len, length...  17.4 us
    slice x6, local copies, waits for them, and re-layouts, scaled_windows(): tiled[:, :window_len * length].reshape(rows, window_len, length)  15.6 us
    all_to_all x1, starting transfers between devices, sent_to_all(): return lax.all_to_all(copies, axis, split_axis=0, concat_axis=0, tiled=True)  9.45 us
  transfers between devices with their start and end apart: 4, of which 3 were waited for; matrix products, arithmetic and copies ran while one was open for 36% of the time, Pallas kernels for 0%

commit v1 on v0

v1 whole, which is shorter than its diff:
```python
import math

import jax
import jax.numpy as jnp
from jax import lax
from jax.experimental import pallas as pl
from jax.experimental.pallas import tpu as pltpu
from jax.sharding import PartitionSpec as P

W = 200
WP = 208
NB = 3
LO = 2048
C = 12
LB = 2304
K = 256
KD = C * WP
NS = 256
NC = NB * NS
EPS = 1e-06
MESH = pl.DeviceIdType.MESH

A = (0, 112)
AH = ((0, 64), (64, 112))
B = (112, 256)
BH = ((192, 256), (112, 192))
F32 = jnp.float32
BF16 = jnp.bfloat16


def rows(span, base=0):
    return pl.ds(span[0] - base, span[1] - span[0])


def kernel(
    owners_ref, data_ref, tmpl_ref, out_ref,
    arch, shifts, base, inv, win, part, y_out, y_in, xo, xi, yb_out, yb_in,
    g_send, g_recv, y_send, y_recv, x_send, x_recv,
):
    tm = lax.axis_index("tmpl")
    ch = lax.axis_index("chan")
    z, yh, core = tm // 4, lax.rem(tm // 2, 2), lax.rem(tm, 2)
    yl, x = ch // 4, lax.rem(ch, 4)

    def tmpl_at(dz, dyh, dcore):
        return lax.rem(z + dz, 4) * 4 + lax.rem(yh + dyh, 2) * 2 + lax.rem(core + dcore, 2)

    def chan_at(dyl, dx):
        return lax.rem(yl + dyl, 2) * 4 + lax.rem(x + dx, 4)

    hops = [(dz, dyh) for dz in range(4) for dyh in range(2) if dz or dyh]
    x_dev = {-1: {"tmpl": tm, "chan": chan_at(0, 3)}, 1: {"tmpl": tm, "chan": chan_at(0, 1)}}
    y_dev = {"tmpl": tm, "chan": chan_at(1, 0)}
    mate = {"tmpl": tmpl_at(0, 0, 1), "chan": ch}

    barrier = pltpu.get_barrier_semaphore()
    peers = [mate, y_dev, x_dev[-1], x_dev[1]]
    peers += [{"tmpl": tmpl_at(dz, dyh, 0), "chan": ch} for dz, dyh in hops]
    for peer in peers:
        pl.semaphore_signal(barrier, inc=1, device_id=peer, device_id_type=MESH)
    pl.semaphore_wait(barrier, len(peers))

    sends = []
    for n, (dz, dyh) in enumerate(hops):
        copy = pltpu.make_async_remote_copy(
            data_ref, arch.at[tm], g_send.at[n], g_recv.at[n],
            device_id={"tmpl": tmpl_at(dz, dyh, 0), "chan": ch}, device_id_type=MESH)
        copy.start()
        sends.append(copy)
    copy = pltpu.make_async_remote_copy(
        data_ref, arch.at[tm], g_send.at[7], g_recv.at[7], device_id=mate, device_id_type=MESH)
    copy.start()
    sends.append(copy)
    arch[tm] = data_ref[...]
    forwards = []
    for n, (dz, dyh) in enumerate(hops):
        source = tmpl_at((4 - dz) % 4, dyh, 0)
        sends[n].wait_recv()
        copy = pltpu.make_async_remote_copy(
            arch.at[source], arch.at[source], g_send.at[8 + n], g_recv.at[8 + n],
            device_id=mate, device_id_type=MESH)
        copy.start()
        forwards.append(copy)
    for copy in sends[7:] + forwards:
        copy.wait_recv()

    for b in range(NB):
        seg = arch[owners_ref[b]].astype(F32)
        seg = jnp.concatenate([seg, jnp.zeros((4, LB), F32)], axis=0)
        for s in range(16):
            turned = pltpu.roll(seg, LB - s, 1) if s else seg
            for n in range(LB // 128):
                shifts[n, s * 48 + b * 16 : s * 48 + b * 16 + 16, :] = (
                    turned[:, n * 128 : n * 128 + 128])
        sums = {1: seg * seg}
        for n in (1, 2, 4, 8, 16, 32, 64):
            sums[2 * n] = sums[n] + pltpu.roll(sums[n], LB - n, 1)
        energy = (sums[128] + pltpu.roll(sums[64], LB - 128, 1)
                  + pltpu.roll(sums[8], LB - 192, 1))[:, :LO]
        inv[b] = 1.0 / (jnp.sqrt(energy * (1.0 / W) + EPS) * math.sqrt(W))
    for b in range(NB):
        for c in range(C):
            for n in range(LB // 128):
                base[b * C + c, :, n * 128 : n * 128 + 128] = (
                    shifts[n, pl.ds(b * 16 + c, 16, stride=48), :].astype(BF16))

    def remote(src, dst, send, recv, device):
        return pltpu.make_async_remote_copy(
            src, dst, send, recv, device_id=device, device_id_type=MESH)

    def y_copy(n):
        return remote(y_out.at[n], y_in.at[n], y_send.at[n], y_recv.at[n], y_dev)

    def yb_copy():
        return remote(yb_out, yb_in, y_send.at[4], y_recv.at[4], y_dev)

    def x_span(t, half):
        return AH[half] if t == 2 else BH[half]

    def x_copy(t, kind, half):
        span = rows(x_span(t, half))
        direction = -1 if half == 0 else 1
        if kind == 2:
            direction = -direction
        n = (t * 3 + kind) * 2 + half
        slot = min(t, 1) if t < 2 else 0
        return remote(
            xo.at[slot, kind, span], xi.at[slot, kind, span],
            x_send.at[n], x_recv.at[n], x_dev[direction])

    def x_slot(t):
        return min(t, 1) if t < 2 else 0

    def x_put(t, kind, half, value):
        xo[x_slot(t), kind, rows(x_span(t, half))] = value.astype(BF16)
        x_copy(t, kind, half).start()

    def x_got(t, kind, half):
        x_copy(t, kind, half).wait_recv()
        return xi[x_slot(t), kind, rows(x_span(t, half))].astype(F32)

    def own(n, span):
        return part[n, rows(span)]

    def local(t, n, half):
        span = x_span(t, half)
        if t == 2:
            return own(n, span) + y_in[n - 4, rows(span)].astype(F32)
        return own(n, span)

    def send_far(t, n):
        for half in (0, 1):
            x_put(t, 0, half, local(t, n, half))

    def send_direct(t, n, half):
        x_put(t, 2, half, local(t, n, half))

    def send_relay(t, n, half):
        x_put(t, 1, half, local(t, n, half) + x_got(t, 0, half))

    def total(t, n, half):
        return local(t, n, half) + x_got(t, 1, half) + x_got(t, 2, half)

    def y_first(n):
        y_out[n] = own(n, A).astype(BF16)
        y_copy(n).start()

    def after_0():
        y_first(0)
        send_far(0, 0)

    def after_1():
        y_first(1)
        send_direct(0, 1, 0)

    def after_2():
        y_first(2)
        send_direct(0, 2, 1)
        send_relay(0, 1, 1)
        send_relay(0, 2, 0)

    def after_3():
        y_first(3)

    def after_4():
        send_far(1, 4)
        y_copy(0).wait_recv()
        send_far(2, 4)

    def after_5():
        send_direct(1, 5, 0)
        y_copy(1).wait_recv()
        send_direct(2, 5, 0)
        for half in (0, 1):
            yb_out[rows(x_span(0, half), B[0])] = total(0, 3, half).astype(BF16)
        yb_copy().start()

    def after_6():
        send_direct(1, 6, 1)
        y_copy(2).wait_recv()
        send_direct(2, 6, 1)
        send_relay(1, 5, 1)
        send_relay(1, 6, 0)
        send_relay(2, 5, 1)
        send_relay(2, 6, 0)

    actions = [after_0, after_1, after_2, after_3, after_4, after_5, after_6]

    def chunk(n, carry):
        step = lax.rem(n, 4)
        dx = jnp.where(step == 0, 2, jnp.where(step == 1, 1, jnp.where(step == 2, 3, 0)))
        dest = lax.rem(yl + 1 + n // 4, 2) * 4 + lax.rem(x + dx, 4)
        lag = pl.multiple_of(dest * NS, NS)

        def channel(c, carry):
            row = pl.multiple_of(c * WP, 16)
            for b in range(NB):
                cols = slice(b * NS, (b + 1) * NS)
                wide = base[b * C + c, :, pl.ds(lag, 512)]
                scale = inv[b, pl.ds(c, 1), pl.ds(lag, NS)]
                for r in range(8):
                    turned = pltpu.roll(wide, 512 - 16 * r, 1) if r else wide
                    turned = turned.astype(F32)
                    win[pl.ds(row + 16 * r, 16), cols] = (turned[:, :NS] * scale).astype(BF16)
                    if r < 5:
                        win[pl.ds(row + 16 * r + 128, 16), cols] = (
                            turned[:, 128 : 128 + NS] * scale).astype(BF16)
            return carry

        lax.fori_loop(0, C, channel, 0)
        part[n] = jnp.dot(tmpl_ref[...], win[...], preferred_element_type=F32)
        for m, action in enumerate(actions):
            pl.when(n == m)(action)
        return carry

    lax.fori_loop(0, 8, chunk, 0)

    y_copy(3).wait_recv()
    for half in (0, 1):
        out_ref[rows(AH[half])] = total(2, 7, half)
    yb_copy().wait_recv()
    for half in (0, 1):
        span = x_span(1, half)
        out_ref[rows(span)] = total(1, 7, half) + yb_in[rows(span, B[0])].astype(F32)

    for copy in sends + forwards:
        copy.wait_send()
    for n in range(4):
        y_copy(n).wait_send()
    yb_copy().wait_send()
    for t in range(3):
        for kind in range(3):
            for half in (0, 1):
                x_copy(t, kind, half).wait_send()


def normalize_templates(templates):
    values = templates.astype(F32)
    spread = jnp.sqrt(jnp.mean(values * values, axis=-1, keepdims=True) + EPS)
    scaled = (values / (spread * math.sqrt(W))).astype(BF16)
    return jnp.pad(scaled, ((0, 0), (0, 0), (0, WP - W))).reshape(K, KD)


def body(data, templates, counts, owners):
    normed = normalize_templates(templates)
    vmem = pl.BlockSpec(memory_space=pltpu.VMEM)
    dma = pltpu.SemaphoreType.DMA
    traces = pl.pallas_call(
        kernel,
        out_shape=jax.ShapeDtypeStruct((K, NC), F32),
        in_specs=[pl.BlockSpec(memory_space=pltpu.SMEM), vmem, vmem],
        out_specs=vmem,
        scratch_shapes=[
            pltpu.VMEM((16, C, LB), BF16),
            pltpu.VMEM((LB // 128, 16 * 48, 128), F32),
            pltpu.VMEM((NB * C, 16, LB), BF16),
            pltpu.VMEM((NB, 16, LO), F32),
            pltpu.VMEM((KD, NC), BF16),
            pltpu.VMEM((8, K, NC), F32),
            pltpu.VMEM((4, A[1], NC), BF16),
            pltpu.VMEM((4, A[1], NC), BF16),
            pltpu.VMEM((2, 3, K, NC), BF16),
            pltpu.VMEM((2, 3, K, NC), BF16),
            pltpu.VMEM((B[1] - B[0], NC), BF16),
            pltpu.VMEM((B[1] - B[0], NC), BF16),
            dma((15,)), dma((15,)), dma((5,)), dma((5,)), dma((18,)), dma((18,)),
        ],
        compiler_params=pltpu.CompilerParams(
            collective_id=0, has_side_effects=True, vmem_limit_bytes=60 << 20),
    )(owners, data[0], normed)
    live = jnp.arange(K, dtype=jnp.int32) < counts[0]
    return jnp.where(live[:, None, None], traces.reshape(K, NB, NS), 0.0)


def solution(mesh):
    placed = (P("tmpl", "chan", None), P("tmpl", "chan", None), P("tmpl"), P())
    return jax.shard_map(
        body, mesh=mesh, in_specs=placed, out_specs=P("tmpl", None, "chan"), check_vma=False
    )
```

time: 455 us -> 64.3 us (0.14); the launches traced: 446 us -> 64.1 us
  local copies, waits for them, and re-layouts: 196 us -> 4.23 us
  waiting for transfers between devices: 142 us -> 0 us
  Pallas kernels: 0 us -> 57.1 us
  other arithmetic: 45 us -> 2.02 us
  matrix products: 33.6 us -> 0 us
  between operations: 20 us -> 0.71 us
  starting transfers between devices: 9.57 us -> 0 us
    reduce_scatter x3 -> x0, waiting for transfers between devices: 135 us -> none  [channel_sum(): lax.psum_scatter(partial_value, 'chan', scatter_dimension=1, tiled=True)]
    another operation x9 -> x0, local copies, waits for them, and re-layouts: 115 us -> none  [the longest x6 115 us: scaled_windows(): tiled = jnp.tile(segment[:, :period], (1, window_len + 1))]
    pallas_call x0 -> x1, Pallas kernels: none -> 57.1 us  [body(): pl.pallas_call(kernel, out_shape=jax.ShapeDtypeStruct((K, NC), F32), in_s...]
    unnamed x15 -> x2, local copies, waits for them, and re-layouts: 42 us -> 0.01 us
    convert_element_type x4 -> x1, other arithmetic: 35.1 us -> 0.29 us  [normalize_templates(): scaled = (values / (spread * math.sqrt(W))).astype(BF16)]
    dot_general x6 -> x0, matrix products: 33.6 us -> none  [local_step(): product = jnp.dot(tpl_rows, scaled, preferred_element_type=jnp.float32)]
    slice x7 -> x0, local copies, waits for them, and re-layouts: 17.1 us -> none  [the longest x6 15.6 us: scaled_windows(): tiled[:, :window_len * length].reshape(rows, window_len, length)]
    reshape x3 -> x1, local copies, waits for them, and re-layouts: 17.4 us -> 1.6 us  [normalize_templates(): return jnp.pad(scaled, ((0, 0), (0, 0), (0, WP - W))).reshape(K, KD)]
  transfers between devices with their start and end apart: 4 -> 0, of which waited for: 3 -> 0; matrix products, arithmetic and copies ran while one was open for 36% -> 0% of each run, Pallas kernels for 0% -> 0%
where the time goes in v1:
time: 64.3 us; the launch traced here: 64.1 us
  Pallas kernels  57.1 us (89%)
  local copies, waits for them, and re-layouts  4.23 us (7%)
  other arithmetic  2.02 us (3%)
  between operations  0.71 us (1%)
    pallas_call x1, Pallas kernels, body(): pl.pallas_call(kernel, out_shape=jax.ShapeDtypeStruct((K, NC), F32), in_s...  57.1 us
    reduce_sum x1, other arithmetic, normalize_templates(): spread = jnp.sqrt(jnp.mean(values * values, axis=-1, keepdims=True) + EPS)  1.65 us
    reshape x1, local copies, waits for them, and re-layouts, normalize_templates(): return jnp.pad(scaled, ((0, 0), (0, 0), (0, WP - W))).reshape(K, KD)  1.6 us
    pallas_call x1, local copies, waits for them, and re-layouts, body(): pl.pallas_call(kernel, out_shape=jax.ShapeDtypeStruct((K, NC), F32), in_s...  1.4 us

profile of v1, /device:TPU:1, one launch (start us, length us, event | category | flops | bytes accessed | tf_op | source)
XLA Modules:
  0.0 64.1 jit_solution(16859947057629366157)
XLA Ops:
  0.0 0.0 copy-start
  0.0 1.6 %fusion = f32[256,12]{0,1:T(8,128)S(1)} fusion(bf16[256,12,200]{0,2,1:T(8,128)(2,1)} %param.5), kind=kLoop, calls=%fused_computation.2 | loop fusion | flops 1840128 | bytes 1241088 | tf_op jit(solution)/shard_map/reduce_sum | solution.py:259
  1.7 0.0 copy-done
  1.7 0.3 fusion.1
  2.0 0.1 pad.4
  2.1 1.6 %copy.7.tmpl_ref = bf16[256,2496]{1,0:T(8,128)(2,1)} copy(bf16[256,2496]{0,1:T(8,128)(2,1)S(1)} %bitcast.5) | data formatting | bytes 2555904 | tf_op jit(solution)/shard_map/reshape | solution.py:261
  3.7 57.1 %shard_map.46 = f32[256,768]{1,0:T(8,128)} custom-call(s32[3]{0:T(128)} %owners_ref.1, bf16[12,2304]{1,0:T(8,128)(2,1)} %bitcast.7, bf16[256,2496]{1,0:T(8,128)(2,1)} %copy.7.tmpl_ref), custom_call_target="tpu_custom_call" | custom-call | tf_op jit(solution)/shard_map/pallas_call | solution.py:268
  60.8 1.4 %copy.8 = f32[256,768]{0,1:T(8,128)S(1)} copy(f32[256,768]{1,0:T(8,128)} %shard_map.46) | data formatting | bytes 1572864 | tf_op jit(solution)/shard_map/pallas_call | solution.py:268
  62.9 0.1 broadcast_select_fusion
  62.9 1.1 %copy.9 = f32[256,3,256]{2,0,1:T(8,128)} copy(f32[256,3,256]{0,2,1:T(8,128)S(1)} %broadcast_select_fusion) | data formatting | bytes 1572864 | tf_op jit(solution)/shard_map/jit(_where)/select_n | solution.py:292
  (2 shorter events, 0.0 us)
Async XLA Ops:
  0.0 1.7 %copy-start = (bf16[256,12,200]{0,2,1:T(8,128)(2,1)S(1)}, bf16[256,12,200]{0,2,1:T(8,128)(2,1)}, u32[]{:S(2)}) copy-start(bf16[256,12,200]{0,2,1:T(8,128)(2,1)} %param.5) | copy-start | bytes 3686404

commit v2 on v1

v2 whole, which is shorter than its diff:
```python
import math

import jax
import jax.numpy as jnp
from jax import lax
from jax.experimental import pallas as pl
from jax.experimental.pallas import tpu as pltpu
from jax.sharding import PartitionSpec as P

W = 200
WP = 208
NB = 3
LO = 2048
C = 12
CH = C // 2
LB = 2304
K = 256
KH = CH * WP
NS = 256
NC = NB * NS
EPS = 1e-06
MESH = pl.DeviceIdType.MESH
GROUPS = (512, 1280, 1280)

A = (0, 112)
AH = ((0, 64), (64, 112))
B = (112, 256)
BH = ((192, 256), (112, 192))
F32 = jnp.float32
BF16 = jnp.bfloat16


def rows(span, base=0):
    return pl.ds(span[0] - base, span[1] - span[0])


def kernel(
    owners_ref, data_ref, tmpl_ref, out_ref,
    arch0, arch1, arch2, columns, lhs0, lhs1, shifts, base, inv, win0, win1, part,
    y_out, y_in, xo, xi, yb_out, yb_in,
    g_send, g_recv, y_send, y_recv, x_send, x_recv,
):
    tm = lax.axis_index("tmpl")
    ch = lax.axis_index("chan")
    z, yh, core = tm // 4, lax.rem(tm // 2, 2), lax.rem(tm, 2)
    yl, x = ch // 4, lax.rem(ch, 4)
    e = 1 - 2 * core

    def block(dz, dyh):
        return lax.rem(z + 4 + dz * e, 4) * 4 + lax.rem(yh + dyh, 2) * 2 + core

    def chan_at(dyl, dx):
        return lax.rem(yl + dyl, 2) * 4 + lax.rem(x + dx, 4)

    ahead = {"tmpl": block(1, 0), "chan": ch}
    behind = {"tmpl": block(-1, 0), "chan": ch}
    across = {"tmpl": block(0, 1), "chan": ch}
    mate = {"tmpl": z * 4 + yh * 2 + (1 - core), "chan": ch}
    x_dev = {-1: {"tmpl": tm, "chan": chan_at(0, 3)}, 1: {"tmpl": tm, "chan": chan_at(0, 1)}}
    y_dev = {"tmpl": tm, "chan": chan_at(1, 0)}

    barrier = pltpu.get_barrier_semaphore()
    peers = [mate, ahead, behind, across, y_dev, x_dev[-1], x_dev[1]]
    for peer in peers:
        pl.semaphore_signal(barrier, inc=1, device_id=peer, device_id_type=MESH)
    pl.semaphore_wait(barrier, len(peers))

    def remote(src, dst, send, recv, device):
        return pltpu.make_async_remote_copy(
            src, dst, send, recv, device_id=device, device_id_type=MESH)

    archs = (arch0, arch1, arch2)
    first = (1 - yl) * 4 + lax.rem(x + 2, 4)
    starts = [
        pl.multiple_of(first * NS, NS),
        pl.multiple_of((1 - yl) * 1024, 1024),
        pl.multiple_of(yl * 1024, 1024),
    ]
    targets = (ahead, behind, across, ahead, ahead, behind, ahead, mate) + (mate,) * 7
    carried = (None, None, None, (-1, 0), (0, 1), (0, 1), (-1, 1), None)
    carried += ((-1, 0), (1, 0), (0, 1), (-2, 0), (-1, 1), (1, 1), (-2, 1))

    def g_copy(g, m):
        if carried[m] is None:
            src = data_ref.at[:, pl.ds(starts[g], GROUPS[g])]
            dst = archs[g].at[tm]
        else:
            src = dst = archs[g].at[block(*carried[m])]
        return remote(src, dst, g_send.at[g, m], g_recv.at[g, m], targets[m])

    def g_start(g):
        for m in (2, 0, 1, 7):
            g_copy(g, m).start()
        archs[g][tm] = data_ref[:, pl.ds(starts[g], GROUPS[g])]

    def g_pass(g, m, on):
        g_copy(g, m).wait_recv()
        for k in on:
            g_copy(g, k).start()

    def g_stage1(g):
        g_pass(g, 0, (3, 8))
        g_pass(g, 1, (9,))
        g_pass(g, 2, (4, 5, 10))

    def g_stage2(g):
        g_pass(g, 3, (11,))
        g_pass(g, 4, (6, 12))
        g_pass(g, 5, (13,))

    def g_stage3(g):
        g_pass(g, 6, (14,))

    def g_finish(g):
        for m in range(7, 15):
            g_copy(g, m).wait_recv()
        width = GROUPS[g]
        for b in range(NB):
            seg = archs[g][owners_ref[b]].astype(F32)
            seg = jnp.concatenate([seg, jnp.zeros((4, width), F32)], axis=0)
            for s in range(16):
                turned = pltpu.roll(seg, width - s, 1) if s else seg
                for n in range(width // 128):
                    shifts[n, s * 48 + b * 16 : s * 48 + b * 16 + 16, :] = (
                        turned[:, n * 128 : n * 128 + 128])
            sums = {1: seg * seg}
            for n in (1, 2, 4, 8, 16, 32, 64):
                sums[2 * n] = sums[n] + pltpu.roll(sums[n], width - n, 1)
            energy = (sums[128] + pltpu.roll(sums[64], width - 128, 1)
                      + pltpu.roll(sums[8], width - 192, 1))[:, : width - 256]
            inv[b, :, pl.ds(starts[g], width - 256)] = (
                1.0 / (jnp.sqrt(energy * (1.0 / W) + EPS) * math.sqrt(W)))
        for b in range(NB):
            for c in range(C):
                for n in range(width // 128):
                    base[b * C + c, :, pl.ds(starts[g] + n * 128, 128)] = (
                        shifts[n, pl.ds(b * 16 + c, 16, stride=48), :])

    g_start(0)
    g_start(1)

    for half, lhs in ((0, lhs0), (1, lhs1)):
        for c in range(CH):
            values = tmpl_ref[half * CH + c].astype(F32)
            power = jnp.sum(values * values, axis=0, keepdims=True) * (1.0 / W)
            scaled = values * (1.0 / (jnp.sqrt(power + EPS) * math.sqrt(W)))
            columns[c * WP : c * WP + W, :] = scaled
            columns[c * WP + W : (c + 1) * WP, :] = jnp.zeros((WP - W, K), F32)
        lhs[...] = columns[...].T.astype(BF16)

    g_stage1(0)
    g_stage2(0)
    g_stage1(1)
    g_stage3(0)
    g_stage2(1)
    g_start(2)
    g_finish(0)

    def y_copy(n):
        return remote(y_out.at[n], y_in.at[n], y_send.at[n], y_recv.at[n], y_dev)

    def yb_copy():
        return remote(yb_out, yb_in, y_send.at[4], y_recv.at[4], y_dev)

    def x_span(t, half):
        return AH[half] if t == 2 else BH[half]

    def x_slot(t):
        return t % 2

    def x_copy(t, kind, half):
        span = rows(x_span(t, half))
        direction = -1 if half == 0 else 1
        if kind == 2:
            direction = -direction
        n = (t * 3 + kind) * 2 + half
        return remote(
            xo.at[x_slot(t), kind, span], xi.at[x_slot(t), kind, span],
            x_send.at[n], x_recv.at[n], x_dev[direction])

    def x_put(t, kind, half, value):
        xo[x_slot(t), kind, rows(x_span(t, half))] = value.astype(BF16)
        x_copy(t, kind, half).start()

    def x_got(t, kind, half):
        x_copy(t, kind, half).wait_recv()
        return xi[x_slot(t), kind, rows(x_span(t, half))].astype(F32)

    def own(n, span):
        return part[n, rows(span)]

    def local(t, n, half):
        span = x_span(t, half)
        if t == 2:
            return own(n, span) + y_in[n - 4, rows(span)].astype(F32)
        return own(n, span)

    def send_far(t, n):
        for half in (0, 1):
            x_put(t, 0, half, local(t, n, half))

    def send_direct(t, n, half):
        x_put(t, 2, half, local(t, n, half))

    def send_relay(t, n, half):
        x_put(t, 1, half, local(t, n, half) + x_got(t, 0, half))

    def total(t, n, half):
        return local(t, n, half) + x_got(t, 1, half) + x_got(t, 2, half)

    def y_first(n):
        y_out[n] = own(n, A).astype(BF16)
        y_copy(n).start()

    def between_0():
        g_stage3(1)
        g_finish(1)

    def between_1():
        g_stage1(2)

    def between_2():
        g_stage2(2)

    def between_3():
        g_stage3(2)
        g_finish(2)

    def after_0():
        y_first(0)
        send_far(0, 0)

    def after_1():
        y_first(1)
        send_direct(0, 1, 0)

    def after_2():
        y_first(2)
        send_direct(0, 2, 1)

    def after_3():
        y_first(3)

    def after_4():
        send_far(1, 4)
        send_relay(0, 1, 1)
        send_relay(0, 2, 0)

    def after_5():
        send_direct(1, 5, 0)
        y_copy(0).wait_recv()
        send_far(2, 4)

    def after_6():
        send_direct(1, 6, 1)

    betweens = [between_0, between_1, between_2, between_3]
    actions = [after_0, after_1, after_2, after_3, after_4, after_5, after_6]

    def dest(n):
        step = lax.rem(n, 4)
        dx = jnp.where(step == 0, 2, jnp.where(step == 1, 1, jnp.where(step == 2, 3, 0)))
        return lax.rem(yl + 1 + n // 4, 2) * 4 + lax.rem(x + dx, 4)

    def build(win, half, n):
        lag = pl.multiple_of(dest(n) * NS, NS)
        for c in range(CH):
            for b in range(NB):
                cols = slice(b * NS, (b + 1) * NS)
                wide = base[b * C + half * CH + c, :, pl.ds(lag, 512)]
                scale = inv[b, half * CH + c : half * CH + c + 1, pl.ds(lag, NS)]
                for r in range(8):
                    turned = pltpu.roll(wide, 512 - 16 * r, 1) if r else wide
                    row = c * WP + 16 * r
                    win[row : row + 16, cols] = (turned[:, :NS] * scale).astype(BF16)
                    if r < 5:
                        win[row + 128 : row + 144, cols] = (
                            turned[:, 128 : 128 + NS] * scale).astype(BF16)

    build(win0, 0, 0)

    def chunk(n, carry):
        build(win1, 1, n)
        part[n] = jnp.dot(lhs0[...], win0[...], preferred_element_type=F32)
        for m, action in enumerate(betweens):
            pl.when(n == m)(action)
        build(win0, 0, jnp.minimum(n + 1, 7))
        part[n] += jnp.dot(lhs1[...], win1[...], preferred_element_type=F32)
        for m, action in enumerate(actions):
            pl.when(n == m)(action)
        return carry

    lax.fori_loop(0, 8, chunk, 0)

    send_relay(1, 5, 1)
    send_relay(1, 6, 0)
    y_copy(1).wait_recv()
    send_direct(2, 5, 0)
    send_relay(2, 5, 1)
    for half in (0, 1):
        yb_out[rows(x_span(0, half), B[0])] = total(0, 3, half).astype(BF16)
    yb_copy().start()
    y_copy(2).wait_recv()
    send_direct(2, 6, 1)
    send_relay(2, 6, 0)

    def finish(span, value):
        for b in range(NB):
            out_ref[b, rows(span)] = value[:, b * NS : (b + 1) * NS]

    y_copy(3).wait_recv()
    for half in (0, 1):
        finish(AH[half], total(2, 7, half))
    yb_copy().wait_recv()
    for half in (0, 1):
        span = x_span(1, half)
        finish(span, total(1, 7, half) + yb_in[rows(span, B[0])].astype(F32))

    for g in range(3):
        for m in range(15):
            g_copy(g, m).wait_send()
    for n in range(4):
        y_copy(n).wait_send()
    yb_copy().wait_send()
    for t in range(3):
        for kind in range(3):
            for half in (0, 1):
                x_copy(t, kind, half).wait_send()


def body(data, templates, counts, owners):
    vmem = pl.BlockSpec(memory_space=pltpu.VMEM)
    dma = pltpu.SemaphoreType.DMA
    traces = pl.pallas_call(
        kernel,
        out_shape=jax.ShapeDtypeStruct((NB, K, NS), F32),
        in_specs=[pl.BlockSpec(memory_space=pltpu.SMEM), vmem, vmem],
        out_specs=vmem,
        scratch_shapes=[
            pltpu.VMEM((16, C, GROUPS[0]), BF16),
            pltpu.VMEM((16, C, GROUPS[1]), BF16),
            pltpu.VMEM((16, C, GROUPS[2]), BF16),
            pltpu.VMEM((KH, K), F32),
            pltpu.VMEM((K, KH), BF16),
            pltpu.VMEM((K, KH), BF16),
            pltpu.VMEM((GROUPS[1] // 128, 16 * 48, 128), F32),
            pltpu.VMEM((NB * C, 16, LB), F32),
            pltpu.VMEM((NB, 16, LO), F32),
            pltpu.VMEM((KH, NC), BF16),
            pltpu.VMEM((KH, NC), BF16),
            pltpu.VMEM((8, K, NC), F32),
            pltpu.VMEM((4, A[1], NC), BF16),
            pltpu.VMEM((4, A[1], NC), BF16),
            pltpu.VMEM((2, 3, K, NC), BF16),
            pltpu.VMEM((2, 3, K, NC), BF16),
            pltpu.VMEM((B[1] - B[0], NC), BF16),
            pltpu.VMEM((B[1] - B[0], NC), BF16),
            dma((3, 15)), dma((3, 15)), dma((5,)), dma((5,)), dma((18,)), dma((18,)),
        ],
        compiler_params=pltpu.CompilerParams(
            collective_id=0, has_side_effects=True, vmem_limit_bytes=60 << 20),
    )(owners, data[0], jnp.transpose(templates, (1, 2, 0)))
    live = jnp.arange(K, dtype=jnp.int32) < counts[0]
    return jnp.transpose(jnp.where(live[None, :, None], traces, 0.0), (1, 0, 2))


def solution(mesh):
    placed = (P("tmpl", "chan", None), P("tmpl", "chan", None), P("tmpl"), P())
    return jax.shard_map(
        body, mesh=mesh, in_specs=placed, out_specs=P("tmpl", None, "chan"), check_vma=False
    )
```

time: 64.3 us -> 65.2 us (1.014)
  Pallas kernels: 57.1 us -> 62.2 us
  local copies, waits for them, and re-layouts: 4.23 us -> 0 us
    pallas_call x1, Pallas kernels: 57.1 us -> 62.2 us  [body(): pl.pallas_call(kernel, out_shape=jax.ShapeDtypeStruct((NB, K, NS), F32),...]
    transpose x0 -> x1, other arithmetic: none -> 2.13 us  [body(): return jnp.transpose(jnp.where(live[None, :, None], traces, 0.0), (1, 0, 2))]
    reduce_sum x1 -> x0, other arithmetic: 1.65 us -> none  [normalize_templates(): spread = jnp.sqrt(jnp.mean(values * values, axis=-1, keepdims=True) + EPS)]
    reshape x1 -> x0, local copies, waits for them, and re-layouts: 1.6 us -> none  [normalize_templates(): return jnp.pad(scaled, ((0, 0), (0, 0), (0, WP - W))).reshape(K, KD)]
    pallas_call x1 -> x0, local copies, waits for them, and re-layouts: 1.4 us -> none  [body(): pl.pallas_call(kernel, out_shape=jax.ShapeDtypeStruct((K, NC), F32), in_s...]
    select_n x1 -> x0, local copies, waits for them, and re-layouts: 1.15 us -> none  [body(): return jnp.where(live[:, None, None], traces.reshape(K, NB, NS), 0.0)]
where the time goes in v2:
time: 65.2 us; the launch traced here: 65 us
  Pallas kernels  62.2 us (95%)
  other arithmetic  2.14 us (3%)
  between operations  0.67 us (1%)
    pallas_call x1, Pallas kernels, body(): pl.pallas_call(kernel, out_shape=jax.ShapeDtypeStruct((NB, K, NS), F32),...  62.2 us
    transpose x1, other arithmetic, body(): return jnp.transpose(jnp.where(live[None, :, None], traces, 0.0), (1, 0, 2))  2.13 us

profile of v2, /device:TPU:1, one launch (start us, length us, event | category | flops | bytes accessed | tf_op | source)
XLA Modules:
  0.0 65.0 jit_solution(11856862765497313810)
XLA Ops:
  0.7 62.2 %shard_map.46 = f32[3,256,256]{2,1,0:T(8,128)} custom-call(s32[3]{0:T(128)} %owners_ref.1, bf16[12,2304]{1,0:T(8,128)(2,1)} %bitcast.7, bf16[12,200,256]{2,1,0:T(8,128)(2,1)} %bitcast.6), custom_call_target="tpu_custom_call" | custom-call | tf_op jit(solution)/shard_map/pallas_call | solution.py:334
  62.9 2.1 %select_bitcast_fusion = f32[256,3,256]{2,0,1:T(8,128)} fusion(f32[3,256,256]{2,1,0:T(8,128)} %shard_map.46, pred[256]{0:T(512)(128)(4,1)S(1)} %iota_compare_fusion), kind=kLoop, calls=%fused_computation | loop fusion | flops 196608 | bytes 1573120 | tf_op jit(solution)/shard_map/transpose | solution.py:364
  (1 shorter events, 0.0 us)

commit v3 on v2

--- a/solution.py
+++ b/solution.py
@@ -8,14 +8,16 @@
 from jax.sharding import PartitionSpec as P
 
 W = 200
-WP = 208
 NB = 3
 LO = 2048
 C = 12
-CH = C // 2
+CG = C // 4
 LB = 2304
 K = 256
-KH = CH * WP
+KR = 16 * CG
+PHASES = ((0, 16), (16, 32))
+TAPS = tuple(tuple(g for lo in (a, a + 32) for g in range(lo, lo + 16) if 4 * g < W) for a, _ in PHASES)
+KH = tuple(len(taps) * KR for taps in TAPS)
 NS = 256
 NC = NB * NS
 EPS = 1e-06
@@ -36,7 +38,7 @@
 
 def kernel(
     owners_ref, data_ref, tmpl_ref, out_ref,
-    arch0, arch1, arch2, columns, lhs0, lhs1, shifts, base, inv, win0, win1, part,
+    arch0, arch1, arch2, normed, columns, lhs0, lhs1, base, inv, band, win0, win1, part,
     y_out, y_in, xo, xi, yb_out, yb_in,
     g_send, g_recv, y_send, y_recv, x_send, x_recv,
 ):
@@ -118,35 +120,53 @@
         for b in range(NB):
             seg = archs[g][owners_ref[b]].astype(F32)
             seg = jnp.concatenate([seg, jnp.zeros((4, width), F32)], axis=0)
-            for s in range(16):
+            small = seg * (1.0 / 256)
+            power = jnp.minimum(small * small, 2.0**120)
+            high = power.astype(BF16)
+            low = (power - high.astype(F32)).astype(BF16)
+            squares = jnp.concatenate([high, low], axis=0)
+            for n in range(width // NS - 1):
+                energy = jnp.dot(squares[:, n * NS : n * NS + 512], band[...],
+                                 preferred_element_type=F32)
+                mean = (energy[:16] + energy[16:]) * (65536.0 / W)
+                scale = 1.0 / (jnp.sqrt(mean + EPS) * math.sqrt(W))
+                for q in range(CG):
+                    for s in range(4):
+                        inv[b * CG + q, 4 * s : 4 * s + 4, pl.ds(starts[g] + n * NS, NS)] = (
+                            scale[4 * q : 4 * q + 4])
+            seg = seg.astype(BF16)
+            for s in range(4):
                 turned = pltpu.roll(seg, width - s, 1) if s else seg
-                for n in range(width // 128):
-                    shifts[n, s * 48 + b * 16 : s * 48 + b * 16 + 16, :] = (
-                        turned[:, n * 128 : n * 128 + 128])
-            sums = {1: seg * seg}
-            for n in (1, 2, 4, 8, 16, 32, 64):
-                sums[2 * n] = sums[n] + pltpu.roll(sums[n], width - n, 1)
-            energy = (sums[128] + pltpu.roll(sums[64], width - 128, 1)
-                      + pltpu.roll(sums[8], width - 192, 1))[:, : width - 256]
-            inv[b, :, pl.ds(starts[g], width - 256)] = (
-                1.0 / (jnp.sqrt(energy * (1.0 / W) + EPS) * math.sqrt(W)))
-        for b in range(NB):
-            for c in range(C):
-                for n in range(width // 128):
-                    base[b * C + c, :, pl.ds(starts[g] + n * 128, 128)] = (
-                        shifts[n, pl.ds(b * 16 + c, 16, stride=48), :])
+                turned = turned.astype(F32)
+                for q in range(CG):
+                    base[b * CG + q, 4 * s : 4 * s + 4, pl.ds(starts[g], width)] = (
+                        turned[4 * q : 4 * q + 4])
 
     g_start(0)
     g_start(1)
 
-    for half, lhs in ((0, lhs0), (1, lhs1)):
-        for c in range(CH):
-            values = tmpl_ref[half * CH + c].astype(F32)
-            power = jnp.sum(values * values, axis=0, keepdims=True) * (1.0 / W)
-            scaled = values * (1.0 / (jnp.sqrt(power + EPS) * math.sqrt(W)))
-            columns[c * WP : c * WP + W, :] = scaled
-            columns[c * WP + W : (c + 1) * WP, :] = jnp.zeros((WP - W, K), F32)
-        lhs[...] = columns[...].T.astype(BF16)
+    sample = lax.broadcasted_iota(jnp.int32, (512, NS), 0)
+    lag_of = lax.broadcasted_iota(jnp.int32, (512, NS), 1)
+    inside = jnp.logical_and(sample >= lag_of, sample < lag_of + W)
+    band[...] = jnp.where(inside, 1.0, 0.0).astype(BF16)
+
+    for c in range(C):
+        values = tmpl_ref[c].astype(F32)
+        power = jnp.sum(values * values, axis=0, keepdims=True) * (1.0 / W)
+        scaled = values * (1.0 / (jnp.sqrt(power + EPS) * math.sqrt(W)))
+        for j in range(2):
+            normed[j] = scaled[:, j * 128 : j * 128 + 128]
+            for s in range(4):
+                row = c // 4 * 16 + 4 * s + c % 4
+                columns[j, pl.ds(row, W // 4, stride=KR), :] = (
+                    normed[j, pl.ds(s, W // 4, stride=4), :])
+    for lhs, (lo, hi) in ((lhs0, PHASES[0]), (lhs1, PHASES[1])):
+        tail = min(hi + 32, W // 4)
+        for j in range(2):
+            band_rows = slice(j * 128, j * 128 + 128)
+            cut = (hi - lo) * KR
+            lhs[band_rows, :cut] = columns[j, lo * KR : hi * KR, :].T.astype(BF16)
+            lhs[band_rows, cut:] = columns[j, (lo + 32) * KR : tail * KR, :].T.astype(BF16)
 
     g_stage1(0)
     g_stage2(0)
@@ -264,17 +284,20 @@
 
     def build(win, half, n):
         lag = pl.multiple_of(dest(n) * NS, NS)
-        for c in range(CH):
-            for b in range(NB):
-                cols = slice(b * NS, (b + 1) * NS)
-                wide = base[b * C + half * CH + c, :, pl.ds(lag, 512)]
-                scale = inv[b, half * CH + c : half * CH + c + 1, pl.ds(lag, NS)]
-                for r in range(8):
-                    turned = pltpu.roll(wide, 512 - 16 * r, 1) if r else wide
-                    row = c * WP + 16 * r
+        taps = TAPS[half]
+        for b in range(NB):
+            cols = slice(b * NS, (b + 1) * NS)
+            for q in range(CG):
+                wide = base[b * CG + q, :, pl.ds(lag, 512)].astype(BF16)
+                scale = inv[b * CG + q, :, pl.ds(lag, NS)]
+                for p in range(*PHASES[half]):
+                    turned = pltpu.roll(wide, 512 - 4 * p, 1) if p else wide
+                    turned = turned.astype(F32)
+                    row = taps.index(p) * KR + q * 16
                     win[row : row + 16, cols] = (turned[:, :NS] * scale).astype(BF16)
-                    if r < 5:
-                        win[row + 128 : row + 144, cols] = (
+                    if p + 32 in taps:
+                        row = taps.index(p + 32) * KR + q * 16
+                        win[row : row + 16, cols] = (
                             turned[:, 128 : 128 + NS] * scale).astype(BF16)
 
     build(win0, 0, 0)
@@ -340,14 +363,15 @@
             pltpu.VMEM((16, C, GROUPS[0]), BF16),
             pltpu.VMEM((16, C, GROUPS[1]), BF16),
             pltpu.VMEM((16, C, GROUPS[2]), BF16),
-            pltpu.VMEM((KH, K), F32),
-            pltpu.VMEM((K, KH), BF16),
-            pltpu.VMEM((K, KH), BF16),
-            pltpu.VMEM((GROUPS[1] // 128, 16 * 48, 128), F32),
-            pltpu.VMEM((NB * C, 16, LB), F32),
-            pltpu.VMEM((NB, 16, LO), F32),
-            pltpu.VMEM((KH, NC), BF16),
-            pltpu.VMEM((KH, NC), BF16),
+            pltpu.VMEM((2, W, 128), F32),
+            pltpu.VMEM((2, W * C, 128), F32),
+            pltpu.VMEM((K, KH[0]), BF16),
+            pltpu.VMEM((K, KH[1]), BF16),
+            pltpu.VMEM((NB * CG, 16, LB), F32),
+            pltpu.VMEM((NB * CG, 16, LO), F32),
+            pltpu.VMEM((512, NS), BF16),
+            pltpu.VMEM((KH[0], NC), BF16),
+            pltpu.VMEM((KH[1], NC), BF16),
             pltpu.VMEM((8, K, NC), F32),
             pltpu.VMEM((4, A[1], NC), BF16),
             pltpu.VMEM((4, A[1], NC), BF16),

time: 65.2 us -> 59 us (0.905)
  Pallas kernels: 62.2 us -> 56 us
    pallas_call x1, Pallas kernels: 62.2 us -> 56 us  [body(): pl.pallas_call(kernel, out_shape=jax.ShapeDtypeStruct((NB, K, NS), F32),...]
where the time goes in v3:
time: 59 us; the launch traced here: 58.8 us
  Pallas kernels  56 us (95%)
  other arithmetic  2.14 us (4%)
  between operations  0.67 us (1%)
    pallas_call x1, Pallas kernels, body(): pl.pallas_call(kernel, out_shape=jax.ShapeDtypeStruct((NB, K, NS), F32),...  56 us
    transpose x1, other arithmetic, body(): return jnp.transpose(jnp.where(live[None, :, None], traces, 0.0), (1, 0, 2))  2.13 us

profile of v3, /device:TPU:1, one launch (start us, length us, event | category | flops | bytes accessed | tf_op | source)
XLA Modules:
  0.0 58.8 jit_solution(6314946454695750068)
XLA Ops:
  0.7 56.0 %shard_map.46 = f32[3,256,256]{2,1,0:T(8,128)} custom-call(s32[3]{0:T(128)} %owners_ref.1, bf16[12,2304]{1,0:T(8,128)(2,1)} %bitcast.7, bf16[12,200,256]{2,1,0:T(8,128)(2,1)} %bitcast.6), custom_call_target="tpu_custom_call" | custom-call | tf_op jit(solution)/shard_map/pallas_call | solution.py:357
  56.7 2.1 %select_bitcast_fusion = f32[256,3,256]{2,0,1:T(8,128)} fusion(f32[3,256,256]{2,1,0:T(8,128)} %shard_map.46, pred[256]{0:T(512)(128)(4,1)S(1)} %iota_compare_fusion), kind=kLoop, calls=%fused_computation | loop fusion | flops 196608 | bytes 1573120 | tf_op jit(solution)/shard_map/transpose | solution.py:388
  (1 shorter events, 0.0 us)

commit v4 on v3

--- a/solution.py
+++ b/solution.py
@@ -23,6 +23,7 @@
 EPS = 1e-06
 MESH = pl.DeviceIdType.MESH
 GROUPS = (512, 1280, 1280)
+MODES = ("chip", "chip", "tree")
 
 A = (0, 112)
 AH = ((0, 64), (64, 112))
@@ -51,18 +52,24 @@
     def block(dz, dyh):
         return lax.rem(z + 4 + dz * e, 4) * 4 + lax.rem(yh + dyh, 2) * 2 + core
 
+    def holder(dz, dyh, dcore):
+        near = lax.rem(z + dz, 4) * 4 + lax.rem(yh + dyh, 2) * 2 + lax.rem(core + dcore, 2)
+        return {"tmpl": near, "chan": ch}
+
     def chan_at(dyl, dx):
         return lax.rem(yl + dyl, 2) * 4 + lax.rem(x + dx, 4)
 
     ahead = {"tmpl": block(1, 0), "chan": ch}
     behind = {"tmpl": block(-1, 0), "chan": ch}
     across = {"tmpl": block(0, 1), "chan": ch}
-    mate = {"tmpl": z * 4 + yh * 2 + (1 - core), "chan": ch}
+    mate = holder(0, 0, 1)
     x_dev = {-1: {"tmpl": tm, "chan": chan_at(0, 3)}, 1: {"tmpl": tm, "chan": chan_at(0, 1)}}
     y_dev = {"tmpl": tm, "chan": chan_at(1, 0)}
 
     barrier = pltpu.get_barrier_semaphore()
-    peers = [mate, ahead, behind, across, y_dev, x_dev[-1], x_dev[1]]
+    chips = [(dz, dyh) for dyh in range(2) for dz in (2, 1, 3, 0) if dz or dyh]
+    others = [holder(dz, dyh, dcore) for dcore in range(2) for dz, dyh in chips] + [mate]
+    peers = others + [y_dev, x_dev[-1], x_dev[1]]
     for peer in peers:
         pl.semaphore_signal(barrier, inc=1, device_id=peer, device_id_type=MESH)
     pl.semaphore_wait(barrier, len(peers))
@@ -78,20 +85,34 @@
         pl.multiple_of((1 - yl) * 1024, 1024),
         pl.multiple_of(yl * 1024, 1024),
     ]
-    targets = (ahead, behind, across, ahead, ahead, behind, ahead, mate) + (mate,) * 7
+    tree_targets = (ahead, behind, across, ahead, ahead, behind, ahead, mate) + (mate,) * 7
     carried = (None, None, None, (-1, 0), (0, 1), (0, 1), (-1, 1), None)
     carried += ((-1, 0), (1, 0), (0, 1), (-2, 0), (-1, 1), (1, 1), (-2, 1))
 
     def g_copy(g, m):
-        if carried[m] is None:
+        mode = MODES[g]
+        source = None
+        if mode == "all":
+            target = others[m]
+        elif mode == "chip":
+            target = others[m] if m < 7 else mate
+            if m > 7:
+                dz, dyh = chips[m - 8]
+                source = holder((4 - dz) % 4, dyh, 0)["tmpl"]
+        else:
+            target = tree_targets[m]
+            if carried[m] is not None:
+                source = block(*carried[m])
+        if source is None:
             src = data_ref.at[:, pl.ds(starts[g], GROUPS[g])]
             dst = archs[g].at[tm]
         else:
-            src = dst = archs[g].at[block(*carried[m])]
-        return remote(src, dst, g_send.at[g, m], g_recv.at[g, m], targets[m])
+            src = dst = archs[g].at[source]
+        return remote(src, dst, g_send.at[g, m], g_recv.at[g, m], target)
 
     def g_start(g):
-        for m in (2, 0, 1, 7):
+        first = {"all": range(15), "chip": range(8), "tree": (2, 0, 1, 7)}[MODES[g]]
+        for m in first:
             g_copy(g, m).start()
         archs[g][tm] = data_ref[:, pl.ds(starts[g], GROUPS[g])]
 
@@ -101,20 +122,26 @@
             g_copy(g, k).start()
 
     def g_stage1(g):
-        g_pass(g, 0, (3, 8))
-        g_pass(g, 1, (9,))
-        g_pass(g, 2, (4, 5, 10))
+        if MODES[g] == "tree":
+            g_pass(g, 0, (3, 8))
+            g_pass(g, 1, (9,))
+            g_pass(g, 2, (4, 5, 10))
+        if MODES[g] == "chip":
+            for m in (6, 1, 2, 0, 4, 5, 3):
+                g_pass(g, m, (8 + m,))
 
     def g_stage2(g):
-        g_pass(g, 3, (11,))
-        g_pass(g, 4, (6, 12))
-        g_pass(g, 5, (13,))
+        if MODES[g] == "tree":
+            g_pass(g, 3, (11,))
+            g_pass(g, 4, (6, 12))
+            g_pass(g, 5, (13,))
 
     def g_stage3(g):
-        g_pass(g, 6, (14,))
+        if MODES[g] == "tree":
+            g_pass(g, 6, (14,))
 
     def g_finish(g):
-        for m in range(7, 15):
+        for m in range(0 if MODES[g] == "all" else 7, 15):
             g_copy(g, m).wait_recv()
         width = GROUPS[g]
         for b in range(NB):
@@ -144,6 +171,7 @@
 
     g_start(0)
     g_start(1)
+    g_start(2)
 
     sample = lax.broadcasted_iota(jnp.int32, (512, NS), 0)
     lag_of = lax.broadcasted_iota(jnp.int32, (512, NS), 1)
@@ -170,10 +198,7 @@
 
     g_stage1(0)
     g_stage2(0)
-    g_stage1(1)
     g_stage3(0)
-    g_stage2(1)
-    g_start(2)
     g_finish(0)
 
     def y_copy(n):
@@ -232,18 +257,13 @@
         y_out[n] = own(n, A).astype(BF16)
         y_copy(n).start()
 
-    def between_0():
-        g_stage3(1)
-        g_finish(1)
-
     def between_1():
-        g_stage1(2)
+        g_stage2(2)
 
     def between_2():
-        g_stage2(2)
+        g_stage3(2)
 
     def between_3():
-        g_stage3(2)
         g_finish(2)
 
     def after_0():
@@ -274,8 +294,8 @@
     def after_6():
         send_direct(1, 6, 1)
 
-    betweens = [between_0, between_1, between_2, between_3]
-    actions = [after_0, after_1, after_2, after_3, after_4, after_5, after_6]
+    betweens = [between_1, between_2, between_3]
+    actions = [after_1, after_2, after_3, after_4, after_5, after_6]
 
     def dest(n):
         step = lax.rem(n, 4)
@@ -301,19 +321,27 @@
                             turned[:, 128 : 128 + NS] * scale).astype(BF16)
 
     build(win0, 0, 0)
+    build(win1, 1, 0)
+    part[0] = jnp.dot(lhs0[...], win0[...], preferred_element_type=F32)
+    g_stage1(1)
+    part[0] += jnp.dot(lhs1[...], win1[...], preferred_element_type=F32)
+    after_0()
+    g_stage1(2)
+    g_finish(1)
+    build(win0, 0, 1)
 
     def chunk(n, carry):
         build(win1, 1, n)
         part[n] = jnp.dot(lhs0[...], win0[...], preferred_element_type=F32)
         for m, action in enumerate(betweens):
-            pl.when(n == m)(action)
+            pl.when(n == m + 1)(action)
         build(win0, 0, jnp.minimum(n + 1, 7))
         part[n] += jnp.dot(lhs1[...], win1[...], preferred_element_type=F32)
         for m, action in enumerate(actions):
-            pl.when(n == m)(action)
+            pl.when(n == m + 1)(action)
         return carry
 
-    lax.fori_loop(0, 8, chunk, 0)
+    lax.fori_loop(1, 8, chunk, 0)
 
     send_relay(1, 5, 1)
     send_relay(1, 6, 0)

time: 59 us -> 53 us (0.90)
  Pallas kernels: 56 us -> 49.9 us
    pallas_call x1, Pallas kernels: 56 us -> 49.9 us  [body(): pl.pallas_call(kernel, out_shape=jax.ShapeDtypeStruct((NB, K, NS), F32),...]
where the time goes in v4:
time: 53 us; the launch traced here: 52.7 us
  Pallas kernels  49.9 us (94%)
  other arithmetic  2.14 us (4%)
  between operations  0.67 us (1%)
    pallas_call x1, Pallas kernels, body(): pl.pallas_call(kernel, out_shape=jax.ShapeDtypeStruct((NB, K, NS), F32),...  49.9 us
    transpose x1, other arithmetic, body(): return jnp.transpose(jnp.where(live[None, :, None], traces, 0.0), (1, 0, 2))  2.13 us

profile of v4, /device:TPU:1, one launch (start us, length us, event | category | flops | bytes accessed | tf_op | source)
XLA Modules:
  0.0 52.7 jit_solution(2873705438700852533)
XLA Ops:
  0.7 49.9 %shard_map.46 = f32[3,256,256]{2,1,0:T(8,128)} custom-call(s32[3]{0:T(128)} %owners_ref.1, bf16[12,2304]{1,0:T(8,128)(2,1)} %bitcast.7, bf16[12,200,256]{2,1,0:T(8,128)(2,1)} %bitcast.6), custom_call_target="tpu_custom_call" | custom-call | tf_op jit(solution)/shard_map/pallas_call | solution.py:385
  50.6 2.1 %select_bitcast_fusion = f32[256,3,256]{2,0,1:T(8,128)} fusion(f32[3,256,256]{2,1,0:T(8,128)} %shard_map.46, pred[256]{0:T(512)(128)(4,1)S(1)} %iota_compare_fusion), kind=kLoop, calls=%fused_computation | loop fusion | flops 196608 | bytes 1573120 | tf_op jit(solution)/shard_map/transpose | solution.py:416
  (1 shorter events, 0.0 us)

commit v5 on v4

--- a/solution.py
+++ b/solution.py
@@ -69,7 +69,7 @@
     barrier = pltpu.get_barrier_semaphore()
     chips = [(dz, dyh) for dyh in range(2) for dz in (2, 1, 3, 0) if dz or dyh]
     others = [holder(dz, dyh, dcore) for dcore in range(2) for dz, dyh in chips] + [mate]
-    peers = others + [y_dev, x_dev[-1], x_dev[1]]
+    peers = others[:7] + [mate, y_dev, x_dev[-1], x_dev[1]]
     for peer in peers:
         pl.semaphore_signal(barrier, inc=1, device_id=peer, device_id_type=MESH)
     pl.semaphore_wait(barrier, len(peers))
@@ -170,8 +170,8 @@
                         turned[4 * q : 4 * q + 4])
 
     g_start(0)
+    g_start(2)
     g_start(1)
-    g_start(2)
 
     sample = lax.broadcasted_iota(jnp.int32, (512, NS), 0)
     lag_of = lax.broadcasted_iota(jnp.int32, (512, NS), 1)
@@ -277,22 +277,27 @@
     def after_2():
         y_first(2)
         send_direct(0, 2, 1)
+        send_relay(0, 1, 1)
+        send_relay(0, 2, 0)
 
     def after_3():
         y_first(3)
 
     def after_4():
         send_far(1, 4)
-        send_relay(0, 1, 1)
-        send_relay(0, 2, 0)
+        y_copy(0).wait_recv()
+        send_far(2, 4)
 
     def after_5():
         send_direct(1, 5, 0)
-        y_copy(0).wait_recv()
-        send_far(2, 4)
+        y_copy(1).wait_recv()
+        send_direct(2, 5, 0)
 
     def after_6():
         send_direct(1, 6, 1)
+        for half in (0, 1):
+            yb_out[rows(x_span(0, half), B[0])] = total(0, 3, half).astype(BF16)
+        yb_copy().start()
 
     betweens = [between_1, between_2, between_3]
     actions = [after_1, after_2, after_3, after_4, after_5, after_6]
@@ -324,9 +329,9 @@
     build(win1, 1, 0)
     part[0] = jnp.dot(lhs0[...], win0[...], preferred_element_type=F32)
     g_stage1(1)
+    g_stage1(2)
     part[0] += jnp.dot(lhs1[...], win1[...], preferred_element_type=F32)
     after_0()
-    g_stage1(2)
     g_finish(1)
     build(win0, 0, 1)
 
@@ -345,14 +350,9 @@
 
     send_relay(1, 5, 1)
     send_relay(1, 6, 0)
-    y_copy(1).wait_recv()
-    send_direct(2, 5, 0)
-    send_relay(2, 5, 1)
-    for half in (0, 1):
-        yb_out[rows(x_span(0, half), B[0])] = total(0, 3, half).astype(BF16)
-    yb_copy().start()
     y_copy(2).wait_recv()
     send_direct(2, 6, 1)
+    send_relay(2, 5, 1)
     send_relay(2, 6, 0)
 
     def finish(span, value):

time: 53 us -> 48.4 us (0.913)
  Pallas kernels: 49.9 us -> 45.2 us
    pallas_call x1, Pallas kernels: 49.9 us -> 45.2 us  [body(): pl.pallas_call(kernel, out_shape=jax.ShapeDtypeStruct((NB, K, NS), F32),...]
where the time goes in v5:
time: 48.4 us; the launch traced here: 48 us
  Pallas kernels  45.2 us (93%)
  other arithmetic  2.14 us (4%)
  between operations  0.67 us (1%)
    pallas_call x1, Pallas kernels, body(): pl.pallas_call(kernel, out_shape=jax.ShapeDtypeStruct((NB, K, NS), F32),...  45.2 us
    transpose x1, other arithmetic, body(): return jnp.transpose(jnp.where(live[None, :, None], traces, 0.0), (1, 0, 2))  2.13 us

profile of v5, /device:TPU:1, one launch (start us, length us, event | category | flops | bytes accessed | tf_op | source)
XLA Modules:
  0.0 48.0 jit_solution(13225716006890764438)
XLA Ops:
  0.7 45.2 %shard_map.46 = f32[3,256,256]{2,1,0:T(8,128)} custom-call(s32[3]{0:T(128)} %owners_ref.1, bf16[12,2304]{1,0:T(8,128)(2,1)} %bitcast.7, bf16[12,200,256]{2,1,0:T(8,128)(2,1)} %bitcast.6), custom_call_target="tpu_custom_call" | custom-call | tf_op jit(solution)/shard_map/pallas_call | solution.py:385
  45.9 2.1 %select_bitcast_fusion = f32[256,3,256]{2,0,1:T(8,128)} fusion(f32[3,256,256]{2,1,0:T(8,128)} %shard_map.46, pred[256]{0:T(512)(128)(4,1)S(1)} %iota_compare_fusion), kind=kLoop, calls=%fused_computation | loop fusion | flops 196608 | bytes 1573120 | tf_op jit(solution)/shard_map/transpose | solution.py:416
  (1 shorter events, 0.0 us)

commit v6 on v5

--- a/solution.py
+++ b/solution.py
@@ -40,7 +40,7 @@
 def kernel(
     owners_ref, data_ref, tmpl_ref, out_ref,
     arch0, arch1, arch2, normed, columns, lhs0, lhs1, base, inv, band, win0, win1, part,
-    y_out, y_in, xo, xi, yb_out, yb_in,
+    y_out, y_in, xo, xi, yb_out, yb_in, held, held_sem,
     g_send, g_recv, y_send, y_recv, x_send, x_recv,
 ):
     tm = lax.axis_index("tmpl")
@@ -66,6 +66,8 @@
     x_dev = {-1: {"tmpl": tm, "chan": chan_at(0, 3)}, 1: {"tmpl": tm, "chan": chan_at(0, 1)}}
     y_dev = {"tmpl": tm, "chan": chan_at(1, 0)}
 
+    fetch = pltpu.make_async_copy(tmpl_ref, held.at[pl.ds(0, C)], held_sem)
+    fetch.start()
     barrier = pltpu.get_barrier_semaphore()
     chips = [(dz, dyh) for dyh in range(2) for dz in (2, 1, 3, 0) if dz or dyh]
     others = [holder(dz, dyh, dcore) for dcore in range(2) for dz, dyh in chips] + [mate]
@@ -178,12 +180,13 @@
     inside = jnp.logical_and(sample >= lag_of, sample < lag_of + W)
     band[...] = jnp.where(inside, 1.0, 0.0).astype(BF16)
 
+    fetch.wait()
     for c in range(C):
-        values = tmpl_ref[c].astype(F32)
+        values = held[c].astype(F32)
         power = jnp.sum(values * values, axis=0, keepdims=True) * (1.0 / W)
         scaled = values * (1.0 / (jnp.sqrt(power + EPS) * math.sqrt(W)))
         for j in range(2):
-            normed[j] = scaled[:, j * 128 : j * 128 + 128]
+            normed[j, :W] = scaled[:, j * 128 : j * 128 + 128]
             for s in range(4):
                 row = c // 4 * 16 + 4 * s + c % 4
                 columns[j, pl.ds(row, W // 4, stride=KR), :] = (
@@ -385,14 +388,14 @@
     traces = pl.pallas_call(
         kernel,
         out_shape=jax.ShapeDtypeStruct((NB, K, NS), F32),
-        in_specs=[pl.BlockSpec(memory_space=pltpu.SMEM), vmem, vmem],
+        in_specs=[pl.BlockSpec(memory_space=pltpu.SMEM), vmem, pl.BlockSpec(memory_space=pl.ANY)],
         out_specs=vmem,
         scratch_shapes=[
             pltpu.VMEM((16, C, GROUPS[0]), BF16),
             pltpu.VMEM((16, C, GROUPS[1]), BF16),
             pltpu.VMEM((16, C, GROUPS[2]), BF16),
-            pltpu.VMEM((2, W, 128), F32),
-            pltpu.VMEM((2, W * C, 128), F32),
+            pltpu.VMEM((2, W + 32, 128), F32),
+            pltpu.VMEM((2, W * C + 8 * KR, 128), F32),
             pltpu.VMEM((K, KH[0]), BF16),
             pltpu.VMEM((K, KH[1]), BF16),
             pltpu.VMEM((NB * CG, 16, LB), F32),
@@ -407,6 +410,8 @@
             pltpu.VMEM((2, 3, K, NC), BF16),
             pltpu.VMEM((B[1] - B[0], NC), BF16),
             pltpu.VMEM((B[1] - B[0], NC), BF16),
+            pltpu.VMEM((C + 1, W, K), BF16),
+            dma(()),
             dma((3, 15)), dma((3, 15)), dma((5,)), dma((5,)), dma((18,)), dma((18,)),
         ],
         compiler_params=pltpu.CompilerParams(

time: 48.4 us -> 48 us (level)
  no operation moved by 1% of the time
where the time goes in v6:
time: 48 us; the launch traced here: 47.6 us
  Pallas kernels  44.8 us (93%)
  other arithmetic  2.14 us (4%)
  between operations  0.67 us (1%)
    pallas_call x1, Pallas kernels, body(): pl.pallas_call(kernel, out_shape=jax.ShapeDtypeStruct((NB, K, NS), F32),...  44.8 us
    transpose x1, other arithmetic, body(): return jnp.transpose(jnp.where(live[None, :, None], traces, 0.0), (1, 0, 2))  2.13 us

profile of v6, /device:TPU:1, one launch (start us, length us, event | category | flops | bytes accessed | tf_op | source)
XLA Modules:
  0.0 47.6 jit_solution(17425193002184582411)
XLA Ops:
  0.7 44.8 %shard_map.46 = f32[3,256,256]{2,1,0:T(8,128)} custom-call(s32[3]{0:T(128)} %owners_ref.1, bf16[12,2304]{1,0:T(8,128)(2,1)} %bitcast.7, bf16[12,200,256]{2,1,0:T(8,128)(2,1)} %bitcast.6), custom_call_target="tpu_custom_call" | custom-call | tf_op jit(solution)/shard_map/pallas_call | solution.py:388
  45.5 2.1 %select_bitcast_fusion = f32[256,3,256]{2,0,1:T(8,128)} fusion(f32[3,256,256]{2,1,0:T(8,128)} %shard_map.46, pred[256]{0:T(512)(128)(4,1)S(1)} %iota_compare_fusion), kind=kLoop, calls=%fused_computation | loop fusion | flops 196608 | bytes 1573120 | tf_op jit(solution)/shard_map/transpose | solution.py:421
  (1 shorter events, 0.0 us)

commit v7 on v6

--- a/solution.py
+++ b/solution.py
@@ -362,13 +362,13 @@
         for b in range(NB):
             out_ref[b, rows(span)] = value[:, b * NS : (b + 1) * NS]
 
-    y_copy(3).wait_recv()
-    for half in (0, 1):
-        finish(AH[half], total(2, 7, half))
     yb_copy().wait_recv()
     for half in (0, 1):
         span = x_span(1, half)
         finish(span, total(1, 7, half) + yb_in[rows(span, B[0])].astype(F32))
+    y_copy(3).wait_recv()
+    for half in (0, 1):
+        finish(AH[half], total(2, 7, half))
 
     for g in range(3):
         for m in range(15):

time: 48 us -> 47.8 us (level)
  no operation moved by 1% of the time
where the time goes in v7:
time: 47.8 us; the launch traced here: 47.5 us
  Pallas kernels  44.7 us (94%)
  other arithmetic  2.14 us (4%)
  between operations  0.67 us (1%)
    pallas_call x1, Pallas kernels, body(): pl.pallas_call(kernel, out_shape=jax.ShapeDtypeStruct((NB, K, NS), F32),...  44.7 us
    transpose x1, other arithmetic, body(): return jnp.transpose(jnp.where(live[None, :, None], traces, 0.0), (1, 0, 2))  2.13 us

profile of v7, /device:TPU:1, one launch (start us, length us, event | category | flops | bytes accessed | tf_op | source)
XLA Modules:
  0.0 47.5 jit_solution(3817678984659949425)
XLA Ops:
  0.7 44.7 %shard_map.46 = f32[3,256,256]{2,1,0:T(8,128)} custom-call(s32[3]{0:T(128)} %owners_ref.1, bf16[12,2304]{1,0:T(8,128)(2,1)} %bitcast.7, bf16[12,200,256]{2,1,0:T(8,128)(2,1)} %bitcast.6), custom_call_target="tpu_custom_call" | custom-call | tf_op jit(solution)/shard_map/pallas_call | solution.py:388
  45.4 2.1 %select_bitcast_fusion = f32[256,3,256]{2,0,1:T(8,128)} fusion(f32[3,256,256]{2,1,0:T(8,128)} %shard_map.46, pred[256]{0:T(512)(128)(4,1)S(1)} %iota_compare_fusion), kind=kLoop, calls=%fused_computation | loop fusion | flops 196608 | bytes 1573120 | tf_op jit(solution)/shard_map/transpose | solution.py:421
  (1 shorter events, 0.0 us)
